TPU v7x, 32 devices: a whole 2x2x4 slice. The times are simulated.
32 devices in a mesh: pairs: 2 (over x), src: 8 (over z, y), tgt: 2 (over core).
Axes of the slice: x: 2, y: 2, z: 4, core: 2. Of those that a mesh axis runs over, the one named last changes fastest.
Arguments:
- src_feat: float32 [2048, 32], P(('pairs', 'src'), 'tgt'), parts along dimension 0, may hold values from -0.72 to 0.72
- tgt_feat: float32 [32768, 32], P(('pairs', 'tgt'), 'src'), parts along dimension 0, may hold values from -0.72 to 0.72
- tgt_dual: float32 [32768], P(('pairs', 'tgt')), parts along dimension 0, may hold values from -6 to 6
- core_matrix: float32 [68, 34], P('pairs'), parts along dimension 0, may hold values from -3 to 3
Outputs:
- src_dual: float32 [2048], P(('pairs', 'src')), parts along dimension 0
- tgt_dual_out: float32 [32768], P(('pairs', 'tgt')), parts along dimension 0
- core_out: float32 [68, 34], P('pairs'), parts along dimension 0
There are 2 independent parts, one for each index of `pairs`. A program takes and returns all parts, laid end to end along the dimension named above; each array names one. Nothing has to cross between parts.
All inputs are finite; a program needn't handle non-finite values.
Results may differ from a plain program's by a relative error of at most 0.0003.
Values sent between devices are 32-bit elements; how exact they have to be, the bound alone decides.
No kernel may reach another device: no remote copies, remote signals or barrier semaphores. Data moves between devices by JAX's collectives and lax.ppermute only.
A program may use at most 64 MiB of HBM per device.

v0:
```python
import jax
import jax.numpy as jnp
from jax import lax
from jax.sharding import PartitionSpec as P

OUTER = 2
EPSILON = 0.02
HIGH = lax.Precision.HIGHEST


def merged(array, axis, combine):
    everything = jax.tree.map(lambda part: lax.all_gather(part, axis), array)
    leading = jax.tree.map(lambda part: part[0], everything)

    def step(k, so_far):
        return combine(so_far, jax.tree.map(lambda part: part[k], everything))

    return lax.fori_loop(1, lax.axis_size(axis), step, leading)


def lifted(values):
    squares = jnp.sum(values * values, axis=1, keepdims=True)
    ones = jnp.ones_like(squares)
    left = jnp.concatenate([squares, ones, -2.0 * values], axis=1)
    right = jnp.concatenate([ones, squares, values], axis=1)
    return (left, right)


def merge_logsum(earlier, later):
    top = jnp.maximum(earlier[0], later[0])
    return (top, earlier[1] * jnp.exp(earlier[0] - top) + later[1] * jnp.exp(later[0] - top))


def shards(src_feat, tgt_feat, tgt_dual, core_matrix):
    src_rows = lax.all_gather(src_feat, "tgt", axis=1, tiled=True)
    tgt_rows = lax.all_gather(tgt_feat, "src", axis=1, tiled=True)
    src_left, src_right = lifted(src_rows)
    tgt_left, tgt_right = lifted(tgt_rows)
    src_count = lax.axis_size("src")
    tgt_count = lax.axis_size("tgt")
    row_count = src_rows.shape[0]
    col_count = tgt_rows.shape[0]
    log_src = -jnp.log(jnp.float32(row_count * src_count))
    log_tgt = -jnp.log(jnp.float32(col_count * tgt_count))
    src_dual = jnp.zeros((row_count,), jnp.float32)
    for outer_step in range(OUTER):
        projected = jnp.dot(src_left, core_matrix, precision=HIGH)
        linear = jnp.dot(projected, tgt_right.T, precision=HIGH)
        row_logits = (tgt_dual[None, :] - linear) / EPSILON
        row_max = jnp.max(row_logits, axis=1)
        row_total = jnp.sum(jnp.exp(row_logits - row_max[:, None]), axis=1)
        row_max, row_total = merged((row_max, row_total), "tgt", merge_logsum)
        src_dual = EPSILON * log_src - EPSILON * (row_max + jnp.log(row_total))
        col_logits = (src_dual[:, None] - linear) / EPSILON
        col_max = jnp.max(col_logits, axis=0)
        col_exp = jnp.exp(col_logits - col_max[None, :])
        col_total = jnp.sum(col_exp, axis=0)
        piece_max, piece_total = (
            lax.all_to_all(col_max[None, :], "src", split_axis=1, concat_axis=0, tiled=True),
            lax.all_to_all(col_total[None, :], "src", split_axis=1, concat_axis=0, tiled=True),
        )
        whole_max = jnp.max(piece_max, axis=0)
        whole_total = jnp.sum(piece_total * jnp.exp(piece_max - whole_max[None, :]), axis=0)
        dual_piece = EPSILON * log_tgt - EPSILON * (whole_max + jnp.log(whole_total))
        tgt_dual = lax.all_gather(dual_piece, "src", axis=0, tiled=True)
        coupling = jnp.exp((src_dual[:, None] + tgt_dual[None, :] - linear) / EPSILON)
        weighted = jnp.dot(coupling, tgt_left, precision=HIGH)
        core_part = jnp.dot(src_right.T, weighted, precision=HIGH)
        core_matrix = -2.0 * lax.psum(core_part, ("src", "tgt"))
    return (src_dual, tgt_dual, core_matrix)


def solution(mesh):
    placed = (
        P(("pairs", "src"), "tgt"),
        P(("pairs", "tgt"), "src"),
        P(("pairs", "tgt")),
        P("pairs", None),
    )
    return jax.shard_map(
        shards,
        mesh=mesh,
        in_specs=placed,
        out_specs=(P(("pairs", "src")), P(("pairs", "tgt")), P("pairs", None)),
        check_vma=False,
    )
```

profile of v0, /device:TPU:0, one launch (start us, length us, event | category | flops | bytes accessed | tf_op | source)
XLA Modules:
  0.0 312.0 jit_solution(1951934580604606527)
XLA Ops:
  7.2 0.7 all-gather.11.cloned.1.call-update
  7.9 2.2 all_gather.36
  10.4 42.7 %all-gather.11.cloned.1.call-done = f32[8,4,8192]{2,1,0:T(4,128)} async-done(((f32[1,4,8192]{2,1,0:T(4,128)}), f32[8,4,8192]{2,1,0:T(4,128)}) %all-gather.11.cloned.1.call-update) | async-done | bytes 1048592 | tf_op jit(solution)/shard_map/all_gather | solution.py:36
  53.2 1.6 reshape.132
  55.0 3.8 %fusion.10 = (f32[128]{0:T(128)S(1)}, f32[128,8192]{1,0:T(8,128)S(1)}) fusion(f32[8192]{0:T(1024)S(1)} %copy-done.3, f32[128,34]{1,0:T(8,128)S(1)} %fusion.32, f32[8192,32]{0,1:T(8,128)S(1)} %bitcast.89, f32[8192,1]{0,1:T(1,128)S(1)} %bitcast.91, f32[8192,1]{0,1:T(1,128)S(1)} %broadcast_in_dim.10), kind=kOutput, calls=%fused_computation.18 | convolution fusion | flops 431521664 | bytes 5359104 | tf_op jit(solution)/shard_map/dot_general | solution.py:48
  58.8 1.0 exponential_reduce_fusion.3
  59.8 1.8 all-gather.6
  61.6 1.8 all-gather.5
  63.4 1.2 fusion.11
  64.5 3.3 %all-to-all-start = ((f32[1,8,1024]{2,0,1:T(1,128)}), f32[1,8,1024]{2,0,1:T(1,128)S(1)}, u32[]{:S(2)}, u32[]{:S(2)}) async-start(f32[1,8,1024]{2,0,1:T(1,128)} %bitcast.11), calls=%async_computation | async-start | bytes 65536 | tf_op jit(solution)/shard_map/all_to_all | solution.py:59
  67.9 3.7 %exponential_reduce_fusion.2 = f32[8192]{0:T(1024)} fusion(f32[128,8192]{1,0:T(8,128)} %copy-done.2, f32[8192]{0:T(1024)} %fusion.11, f32[128]{0:T(128)S(1)} %multiply_subtract_fusion.3), kind=kLoop, calls=%fused_computation.14 | loop fusion | flops 4186112 | bytes 4260352 | tf_op jit(solution)/shard_map/reduce_sum | solution.py:57
  71.6 2.9 all-to-all-done
  74.6 3.3 %all-to-all-start.1 = ((f32[1,8,1024]{2,0,1:T(1,128)}), f32[1,8,1024]{2,0,1:T(1,128)S(1)}, u32[]{:S(2)}, u32[]{:S(2)}) async-start(f32[1,8,1024]{2,0,1:T(1,128)} %bitcast.12), calls=%async_computation.1 | async-start | bytes 65536 | tf_op jit(solution)/shard_map/all_to_all | solution.py:60
  77.9 6.6 %all-to-all-done.1 = f32[1,8,1024]{2,0,1:T(1,128)S(1)} async-done(((f32[1,8,1024]{2,0,1:T(1,128)}), f32[1,8,1024]{2,0,1:T(1,128)S(1)}, u32[]{:S(2)}, u32[]{:S(2)}) %all-to-all-start.1) | async-done | bytes 32800 | tf_op jit(solution)/shard_map/all_to_all | solution.py:60
  84.6 30.6 %all_gather.42 = f32[8192]{0:T(1024)S(1)} all-gather(f32[1024]{0:T(1024)S(1)} %multiply_subtract_fusion.1), channel_id=1, replica_groups=mesh['pairs'=2,'src'=8,'tgt'=2] {'src'}, dimensions={0}, use_global_device_ids=true | all-gather | bytes 36864 | tf_op jit(solution)/shard_map/all_gather | solution.py:65
  115.2 6.2 %fusion.5 = f32[128,34]{1,0:T(8,128)S(1)} fusion(f32[128,8192]{1,0:T(8,128)} %copy-done.2, f32[8192]{0:T(1024)S(1)} %all_gather.42, f32[128]{0:T(128)S(1)} %multiply_subtract_fusion.3, f32[8192,32]{0,1:T(8,128)S(1)} %get-tuple-element.27, f32[8192,1]{0,1:T(1,128)S(1)} %broadcast_in_dim.10, f32[8192,1]{0,1:T(1,128)S(1)} %bitcast.92), kind=kOutput, calls=%fused_computation.9 | convolution fusion | flops 431521792 | bytes 5359104 | tf_op jit(solution)/shard_map/dot_general | solution.py:67
  121.6 57.8 %psum.14 = f32[34,34]{1,0:T(8,128)S(1)} all-reduce(f32[34,34]{1,0:T(8,128)S(1)} %fusion.31), channel_id=1, replica_groups=mesh['pairs'=2,'src'=8,'tgt'=2] {'src','tgt'}, use_global_device_ids=true, to_apply=%region_8.0 | all-reduce | flops 1156 | bytes 9248 | tf_op jit(solution)/shard_map/psum | solution.py:69
  179.7 3.8 %fusion.12 = (f32[128]{0:T(128)S(1)}, f32[128,8192]{1,0:T(8,128)S(1)}) fusion(f32[8192]{0:T(1024)S(1)} %all_gather.42, f32[128,34]{1,0:T(8,128)S(1)} %fusion.28, f32[8192,32]{0,1:T(8,128)S(1)} %bitcast.90, f32[8192,1]{0,1:T(1,128)S(1)} %bitcast.93, f32[8192,1]{0,1:T(1,128)S(1)} %broadcast_in_dim.10), kind=kOutput, calls=%fused_computation.20 | convolution fusion | flops 431521664 | bytes 5359104 | tf_op jit(solution)/shard_map/dot_general | solution.py:48
  183.5 1.0 exponential_reduce_fusion.1
  184.5 1.8 all-gather.8
  186.3 1.8 all-gather.7
  188.1 1.1 fusion.13
  189.3 3.3 %all-to-all-start.2 = ((f32[1,8,1024]{2,0,1:T(1,128)}), f32[1,8,1024]{2,0,1:T(1,128)S(1)}, u32[]{:S(2)}, u32[]{:S(2)}) async-start(f32[1,8,1024]{2,0,1:T(1,128)} %bitcast.19), calls=%async_computation.2 | async-start | bytes 65536 | tf_op jit(solution)/shard_map/all_to_all | solution.py:59
  192.6 3.7 %exponential_reduce_fusion = f32[8192]{0:T(1024)} fusion(f32[128,8192]{1,0:T(8,128)} %copy-done.1, f32[8192]{0:T(1024)} %fusion.13, f32[128]{0:T(128)S(1)} %multiply_subtract_fusion.2), kind=kLoop, calls=%fused_computation.5 | loop fusion | flops 4186112 | bytes 4260352 | tf_op jit(solution)/shard_map/reduce_sum | solution.py:57
  196.4 2.9 all-to-all-done.2
  199.3 3.3 %all-to-all-start.3 = ((f32[1,8,1024]{2,0,1:T(1,128)}), f32[1,8,1024]{2,0,1:T(1,128)S(1)}, u32[]{:S(2)}, u32[]{:S(2)}) async-start(f32[1,8,1024]{2,0,1:T(1,128)} %bitcast.20), calls=%async_computation.3 | async-start | bytes 65536 | tf_op jit(solution)/shard_map/all_to_all | solution.py:60
  202.7 6.6 %all-to-all-done.3 = f32[1,8,1024]{2,0,1:T(1,128)S(1)} async-done(((f32[1,8,1024]{2,0,1:T(1,128)}), f32[1,8,1024]{2,0,1:T(1,128)S(1)}, u32[]{:S(2)}, u32[]{:S(2)}) %all-to-all-start.3) | async-done | bytes 32800 | tf_op jit(solution)/shard_map/all_to_all | solution.py:60
  209.3 30.6 %all_gather.47 = f32[8192]{0:T(1024)S(1)} all-gather(f32[1024]{0:T(1024)S(1)} %multiply_subtract_fusion), channel_id=1, replica_groups=mesh['pairs'=2,'src'=8,'tgt'=2] {'src'}, dimensions={0}, use_global_device_ids=true | all-gather | bytes 36864 | tf_op jit(solution)/shard_map/all_gather | solution.py:65
  239.9 6.2 %fusion = f32[128,34]{1,0:T(8,128)S(1)} fusion(f32[128,8192]{1,0:T(8,128)} %copy-done.1, f32[8192]{0:T(1024)S(1)} %all_gather.47, f32[128]{0:T(128)S(1)} %multiply_subtract_fusion.2, f32[8192,32]{0,1:T(8,128)S(1)} %get-tuple-element.27, f32[8192,1]{0,1:T(1,128)S(1)} %broadcast_in_dim.10, f32[8192,1]{0,1:T(1,128)S(1)} %bitcast.94), kind=kOutput, calls=%fused_computation | convolution fusion | flops 431521792 | bytes 5359104 | tf_op jit(solution)/shard_map/dot_general | solution.py:67
  246.3 57.6 %psum.15 = f32[34,34]{1,0:T(8,128)S(1)} all-reduce(f32[34,34]{1,0:T(8,128)S(1)} %fusion.30), channel_id=1, replica_groups=mesh['pairs'=2,'src'=8,'tgt'=2] {'src','tgt'}, use_global_device_ids=true, to_apply=%region_15.0 | all-reduce | flops 1156 | bytes 9248 | tf_op jit(solution)/shard_map/psum | solution.py:69
  303.9 0.6 broadcast_multiply_fusion.1
  304.5 0.6 copy.16
  (27 shorter events, 1.4 us)
Async XLA Ops:
  7.2 3.0 copy-start
  7.2 47.8 %copy-start.3 = (f32[8192]{0:T(1024)S(1)}, f32[8192]{0:T(1024)}, u32[]{:S(2)}) copy-start(f32[8192]{0:T(1024)} %param.6) | copy-start | bytes 98308
  7.2 46.0 %all-gather.11.cloned.1.call-start = ((), (), s32[]{:S(2)}) async-start(), calls=%async_computation.4 | async-start | bytes 1179648 | tf_op jit(solution)/shard_map/all_gather | solution.py:36
  58.8 5.8 %copy-start.2 = (f32[128,8192]{1,0:T(8,128)}, f32[128,8192]{1,0:T(8,128)S(1)}, u32[]{:S(2)}) copy-start(f32[128,8192]{1,0:T(8,128)S(1)} %get-tuple-element.38) | copy-start | bytes 12582916
  64.5 10.0 %all-to-all-start = ((f32[1,8,1024]{2,0,1:T(1,128)}), f32[1,8,1024]{2,0,1:T(1,128)S(1)}, u32[]{:S(2)}, u32[]{:S(2)}) async-start(f32[1,8,1024]{2,0,1:T(1,128)} %bitcast.11), calls=%async_computation | async-start | bytes 65536 | tf_op jit(solution)/shard_map/all_to_all | solution.py:59
  74.6 10.0 %all-to-all-start.1 = ((f32[1,8,1024]{2,0,1:T(1,128)}), f32[1,8,1024]{2,0,1:T(1,128)S(1)}, u32[]{:S(2)}, u32[]{:S(2)}) async-start(f32[1,8,1024]{2,0,1:T(1,128)} %bitcast.12), calls=%async_computation.1 | async-start | bytes 65536 | tf_op jit(solution)/shard_map/all_to_all | solution.py:60
  183.5 5.8 %copy-start.1 = (f32[128,8192]{1,0:T(8,128)}, f32[128,8192]{1,0:T(8,128)S(1)}, u32[]{:S(2)}) copy-start(f32[128,8192]{1,0:T(8,128)S(1)} %get-tuple-element.40) | copy-start | bytes 12582916
  188.1 51.8 %copy-start.4 = (f32[128]{0:T(128)}, f32[128]{0:T(128)S(1)}, u32[]{:S(2)}) copy-start(f32[128]{0:T(128)S(1)} %multiply_subtract_fusion.2) | copy-start | bytes 1540
  189.3 10.0 %all-to-all-start.2 = ((f32[1,8,1024]{2,0,1:T(1,128)}), f32[1,8,1024]{2,0,1:T(1,128)S(1)}, u32[]{:S(2)}, u32[]{:S(2)}) async-start(f32[1,8,1024]{2,0,1:T(1,128)} %bitcast.19), calls=%async_computation.2 | async-start | bytes 65536 | tf_op jit(solution)/shard_map/all_to_all | solution.py:59
  199.3 10.0 %all-to-all-start.3 = ((f32[1,8,1024]{2,0,1:T(1,128)}), f32[1,8,1024]{2,0,1:T(1,128)S(1)}, u32[]{:S(2)}, u32[]{:S(2)}) async-start(f32[1,8,1024]{2,0,1:T(1,128)} %bitcast.20), calls=%async_computation.3 | async-start | bytes 65536 | tf_op jit(solution)/shard_map/all_to_all | solution.py:60
Sparse Core Ops, SparseCore 0:
  10.1 42.9 all-gather.10
where the time goes:
time: 313 us; the launch traced here: 312 us
  blocking collectives  186 us (59%)
  waiting for transfers between devices  62.4 us (20%)
  matrix products  21 us (7%)
  between operations  14.2 us (5%)
  starting transfers between devices  13.4 us (4%)
  other arithmetic  12.7 us (4%)
    psum x2, blocking collectives, shards(): core_matrix = -2.0 * lax.psum(core_part, ('src', 'tgt'))  115 us
    all_gather x2, blocking collectives, shards(): tgt_dual = lax.all_gather(dual_piece, 'src', axis=0, tiled=True)  61.2 us
    all_gather x1, waiting for transfers between devices, shards(): tgt_rows = lax.all_gather(tgt_feat, 'src', axis=1, tiled=True)  42.7 us
    all_to_all x2, waiting for transfers between devices, shards(): lax.all_to_all(col_total[None, :], 'src', split_axis=1, concat_axis=0, ti...  13.2 us
    dot_general x2, matrix products, shards(): weighted = jnp.dot(coupling, tgt_left, precision=HIGH)  12.4 us
    dot_general x2, matrix products, shards(): linear = jnp.dot(projected, tgt_right.T, precision=HIGH)  7.61 us
    reduce_sum x2, other arithmetic, shards(): col_total = jnp.sum(col_exp, axis=0)  7.45 us
    all_gather x4, blocking collectives, merged(): everything = jax.tree.map(lambda part: lax.all_gather(part, axis), array)  7.19 us
  transfers between devices with their start and end apart: 5, of which 5 were waited for; matrix products, arithmetic and copies ran while one was open for 3% of the time, Pallas kernels for 0%

commit v1 on v0

--- a/solution.py
+++ b/solution.py
@@ -6,6 +6,18 @@
 OUTER = 2
 EPSILON = 0.02
 HIGH = lax.Precision.HIGHEST
+
+
+def gather_by_bits(value, axis, dim):
+    ways, here, step = (lax.axis_size(axis), lax.axis_index(axis), value.shape[dim])
+    line, have = (value, 1)
+    while have < ways:
+        line = jnp.concatenate(
+            [line, lax.ppermute(line, axis, [(d, (d - have) % ways) for d in range(ways)])],
+            axis=dim,
+        )
+        have = 2 * have
+    return jnp.roll(line, here * step, axis=dim)
 
 
 def merged(array, axis, combine):
@@ -33,7 +45,7 @@
 
 def shards(src_feat, tgt_feat, tgt_dual, core_matrix):
     src_rows = lax.all_gather(src_feat, "tgt", axis=1, tiled=True)
-    tgt_rows = lax.all_gather(tgt_feat, "src", axis=1, tiled=True)
+    tgt_rows = gather_by_bits(tgt_feat, "src", 1)
     src_left, src_right = lifted(src_rows)
     tgt_left, tgt_right = lifted(tgt_rows)
     src_count = lax.axis_size("src")

time: 313 us -> 301 us (0.962)
  between operations: 14.2 us -> 0.84 us
  waiting for transfers between devices: 62.4 us -> 49.2 us
  starting transfers between devices: 13.4 us -> 24.4 us
    all_gather x1 -> x0, waiting for transfers between devices: 42.7 us -> none  [shards(): tgt_rows = lax.all_gather(tgt_feat, 'src', axis=1, tiled=True)]
    ppermute x0 -> x3, waiting for transfers between devices: none -> 30.1 us  [gather_by_bits(): lax.ppermute(line, axis, [(d, (d - have) % ways) for d in range(ways)])]
    ppermute x0 -> x3, starting transfers between devices: none -> 8.03 us  [gather_by_bits(): lax.ppermute(line, axis, [(d, (d - have) % ways) for d in range(ways)])]
  transfers between devices with their start and end apart: 5 -> 7, of which waited for: 5 -> 7; matrix products, arithmetic and copies ran while one was open for 3% -> 3% of each run, Pallas kernels for 0% -> 0%
where the time goes in v1:
time: 301 us; the launch traced here: 300 us
  blocking collectives  186 us (62%)
  waiting for transfers between devices  49.2 us (16%)
  starting transfers between devices  24.4 us (8%)
  matrix products  21 us (7%)
  other arithmetic  15.7 us (5%)
    psum x2, blocking collectives, shards(): core_matrix = -2.0 * lax.psum(core_part, ('src', 'tgt'))  115 us
    all_gather x2, blocking collectives, shards(): tgt_dual = lax.all_gather(dual_piece, 'src', axis=0, tiled=True)  61.2 us
    ppermute x3, waiting for transfers between devices, gather_by_bits(): lax.ppermute(line, axis, [(d, (d - have) % ways) for d in range(ways)])  30.1 us
    all_to_all x2, waiting for transfers between devices, shards(): lax.all_to_all(col_total[None, :], 'src', split_axis=1, concat_axis=0, ti...  13.2 us
    dot_general x2, matrix products, shards(): weighted = jnp.dot(coupling, tgt_left, precision=HIGH)  12.4 us
    all_to_all x2, starting transfers between devices, shards(): lax.all_to_all(col_max[None, :], 'src', split_axis=1, concat_axis=0, tile...  9.7 us
    ppermute x3, starting transfers between devices, gather_by_bits(): lax.ppermute(line, axis, [(d, (d - have) % ways) for d in range(ways)])  8.03 us
    dot_general x2, matrix products, shards(): linear = jnp.dot(projected, tgt_right.T, precision=HIGH)  7.6 us
  transfers between devices with their start and end apart: 7, of which 7 were waited for; matrix products, arithmetic and copies ran while one was open for 3% of the time, Pallas kernels for 0%

profile of v1, /device:TPU:0, one launch (start us, length us, event | category | flops | bytes accessed | tf_op | source)
XLA Modules:
  0.0 300.0 jit_solution(9890548215445477040)
XLA Ops:
  0.6 6.1 %collective-permute-start = (f32[8192,4]{0,1:T(4,128)}, f32[8192,4]{0,1:T(4,128)S(1)}, u32[]{:S(2)}, u32[]{:S(2)}) collective-permute-start(f32[8192,4]{0,1:T(4,128)} %param.5), channel_id=1, source_target_pairs={{0,14},{2,0},{4,2},{6,4},{8,6},{10,8},{12,10},{14,12},{1,15},{3,1}... | collective-permute-start | bytes 393224 | tf_op jit(solution)/shard_map/ppermute | solution.py:16
  6.7 3.1 %collective-permute-done = f32[8192,4]{0,1:T(4,128)S(1)} collective-permute-done((f32[8192,4]{0,1:T(4,128)}, f32[8192,4]{0,1:T(4,128)S(1)}, u32[]{:S(2)}, u32[]{:S(2)}) %collective-permute-start) | collective-permute-done | bytes 131104 | tf_op jit(solution)/shard_map/ppermute | solution.py:16
  10.8 1.5 collective-permute-start.1
  12.2 5.8 %collective-permute-done.1 = f32[8192,8]{0,1:T(8,128)S(1)} collective-permute-done((f32[8192,8]{0,1:T(8,128)S(1)}, f32[8192,8]{0,1:T(8,128)S(1)}, u32[]{:S(2)}, u32[]{:S(2)}) %collective-permute-start.1) | collective-permute-done | bytes 262176 | tf_op jit(solution)/shard_map/ppermute | solution.py:16
  19.5 2.0 all_gather.33
  21.8 21.3 %collective-permute-done.2 = f32[8192,16]{0,1:T(8,128)S(1)} collective-permute-done((f32[8192,16]{0,1:T(8,128)S(1)}, f32[8192,16]{0,1:T(8,128)S(1)}, u32[]{:S(2)}, u32[]{:S(2)}) %collective-permute-start.2) | collective-permute-done | bytes 524320 | tf_op jit(solution)/shard_map/ppermute | solution.py:16
  43.2 2.3 concatenate.29
  45.4 1.1 broadcast_multiply_fusion
  46.7 3.8 %fusion.10 = (f32[128]{0:T(128)S(1)}, f32[128,8192]{1,0:T(8,128)S(1)}) fusion(f32[8192]{0:T(1024)S(1)} %copy-done.4, f32[128,34]{1,0:T(8,128)S(1)} %fusion.32, f32[8192,32]{0,1:T(8,128)S(1)} %get-tuple-element.28, f32[8192,1]{0,1:T(1,128)S(1)} %bitcast.83, f32[8192,1]{0,1:T(1,128)S(1)} %broadcast_in_dim.10), kind=kOutput, calls=%fused_computation.18 | convolution fusion | flops 431521664 | bytes 5359104 | tf_op jit(solution)/shard_map/dot_general | solution.py:60
  51.5 1.8 all-gather.5
  53.3 1.8 all-gather.4
  55.2 1.2 fusion.11
  56.3 6.4 %all-to-all-start = ((f32[1,8,1024]{2,0,1:T(1,128)}), f32[1,8,1024]{2,0,1:T(1,128)S(1)}, u32[]{:S(2)}, u32[]{:S(2)}) async-start(f32[1,8,1024]{2,0,1:T(1,128)} %bitcast.8), calls=%async_computation | async-start | bytes 65536 | tf_op jit(solution)/shard_map/all_to_all | solution.py:71
  62.7 3.7 %exponential_reduce_fusion.2 = f32[8192]{0:T(1024)} fusion(f32[128,8192]{1,0:T(8,128)} %copy-done.2, f32[8192]{0:T(1024)} %fusion.11, f32[128]{0:T(128)S(1)} %multiply_subtract_fusion.3), kind=kLoop, calls=%fused_computation.14 | loop fusion | flops 4186112 | bytes 4260352 | tf_op jit(solution)/shard_map/reduce_sum | solution.py:69
  66.4 3.0 all-to-all-done
  69.4 3.3 %all-to-all-start.1 = ((f32[1,8,1024]{2,0,1:T(1,128)}), f32[1,8,1024]{2,0,1:T(1,128)S(1)}, u32[]{:S(2)}, u32[]{:S(2)}) async-start(f32[1,8,1024]{2,0,1:T(1,128)} %bitcast.9), calls=%async_computation.1 | async-start | bytes 65536 | tf_op jit(solution)/shard_map/all_to_all | solution.py:72
  72.7 6.6 %all-to-all-done.1 = f32[1,8,1024]{2,0,1:T(1,128)S(1)} async-done(((f32[1,8,1024]{2,0,1:T(1,128)}), f32[1,8,1024]{2,0,1:T(1,128)S(1)}, u32[]{:S(2)}, u32[]{:S(2)}) %all-to-all-start.1) | async-done | bytes 32800 | tf_op jit(solution)/shard_map/all_to_all | solution.py:72
  79.4 30.6 %all_gather.38 = f32[8192]{0:T(1024)S(1)} all-gather(f32[1024]{0:T(1024)S(1)} %multiply_subtract_fusion.1), channel_id=1, replica_groups=mesh['pairs'=2,'src'=8,'tgt'=2] {'src'}, dimensions={0}, use_global_device_ids=true | all-gather | bytes 36864 | tf_op jit(solution)/shard_map/all_gather | solution.py:77
  110.0 6.2 %fusion.5 = f32[128,34]{1,0:T(8,128)S(1)} fusion(f32[128,8192]{1,0:T(8,128)} %copy-done.2, f32[8192]{0:T(1024)S(1)} %all_gather.38, f32[128]{0:T(128)S(1)} %multiply_subtract_fusion.3, f32[8192,32]{0,1:T(8,128)S(1)} %copy-done.3, f32[8192,1]{0,1:T(1,128)S(1)} %broadcast_in_dim.10, f32[8192,1]{0,1:T(1,128)S(1)} %bitcast.84), kind=kOutput, calls=%fused_computation.9 | convolution fusion | flops 431521792 | bytes 5359104 | tf_op jit(solution)/shard_map/dot_general | solution.py:79
  116.4 57.8 %psum.14 = f32[34,34]{1,0:T(8,128)S(1)} all-reduce(f32[34,34]{1,0:T(8,128)S(1)} %fusion.31), channel_id=1, replica_groups=mesh['pairs'=2,'src'=8,'tgt'=2] {'src','tgt'}, use_global_device_ids=true, to_apply=%region_8.9 | all-reduce | flops 1156 | bytes 9248 | tf_op jit(solution)/shard_map/psum | solution.py:81
  174.5 3.8 %fusion.12 = (f32[128]{0:T(128)S(1)}, f32[128,8192]{1,0:T(8,128)S(1)}) fusion(f32[8192]{0:T(1024)S(1)} %all_gather.38, f32[128,34]{1,0:T(8,128)S(1)} %fusion.28, f32[8192,32]{0,1:T(8,128)S(1)} %get-tuple-element.28, f32[8192,1]{0,1:T(1,128)S(1)} %bitcast.85, f32[8192,1]{0,1:T(1,128)S(1)} %broadcast_in_dim.10), kind=kOutput, calls=%fused_computation.20 | convolution fusion | flops 431521664 | bytes 5359104 | tf_op jit(solution)/shard_map/dot_general | solution.py:60
  179.3 1.8 all-gather.7
  181.1 1.8 all-gather.6
  182.9 1.1 fusion.13
  184.1 3.3 %all-to-all-start.2 = ((f32[1,8,1024]{2,0,1:T(1,128)}), f32[1,8,1024]{2,0,1:T(1,128)S(1)}, u32[]{:S(2)}, u32[]{:S(2)}) async-start(f32[1,8,1024]{2,0,1:T(1,128)} %bitcast.16), calls=%async_computation.2 | async-start | bytes 65536 | tf_op jit(solution)/shard_map/all_to_all | solution.py:71
  187.4 3.7 %exponential_reduce_fusion = f32[8192]{0:T(1024)} fusion(f32[128,8192]{1,0:T(8,128)} %copy-done.1, f32[8192]{0:T(1024)} %fusion.13, f32[128]{0:T(128)S(1)} %multiply_subtract_fusion.2), kind=kLoop, calls=%fused_computation.5 | loop fusion | flops 4186112 | bytes 4260352 | tf_op jit(solution)/shard_map/reduce_sum | solution.py:69
  191.2 2.9 all-to-all-done.2
  194.1 3.3 %all-to-all-start.3 = ((f32[1,8,1024]{2,0,1:T(1,128)}), f32[1,8,1024]{2,0,1:T(1,128)S(1)}, u32[]{:S(2)}, u32[]{:S(2)}) async-start(f32[1,8,1024]{2,0,1:T(1,128)} %bitcast.17), calls=%async_computation.3 | async-start | bytes 65536 | tf_op jit(solution)/shard_map/all_to_all | solution.py:72
  197.4 6.6 %all-to-all-done.3 = f32[1,8,1024]{2,0,1:T(1,128)S(1)} async-done(((f32[1,8,1024]{2,0,1:T(1,128)}), f32[1,8,1024]{2,0,1:T(1,128)S(1)}, u32[]{:S(2)}, u32[]{:S(2)}) %all-to-all-start.3) | async-done | bytes 32800 | tf_op jit(solution)/shard_map/all_to_all | solution.py:72
  204.1 30.6 %all_gather.43 = f32[8192]{0:T(1024)S(1)} all-gather(f32[1024]{0:T(1024)S(1)} %multiply_subtract_fusion), channel_id=1, replica_groups=mesh['pairs'=2,'src'=8,'tgt'=2] {'src'}, dimensions={0}, use_global_device_ids=true | all-gather | bytes 36864 | tf_op jit(solution)/shard_map/all_gather | solution.py:77
  234.7 6.2 %fusion = f32[128,34]{1,0:T(8,128)S(1)} fusion(f32[128,8192]{1,0:T(8,128)} %copy-done.1, f32[8192]{0:T(1024)S(1)} %all_gather.43, f32[128]{0:T(128)S(1)} %multiply_subtract_fusion.2, f32[8192,32]{0,1:T(8,128)S(1)} %copy-done.3, f32[8192,1]{0,1:T(1,128)S(1)} %broadcast_in_dim.10, f32[8192,1]{0,1:T(1,128)S(1)} %bitcast.86), kind=kOutput, calls=%fused_computation | convolution fusion | flops 431521792 | bytes 5359104 | tf_op jit(solution)/shard_map/dot_general | solution.py:79
  241.1 57.6 %psum.15 = f32[34,34]{1,0:T(8,128)S(1)} all-reduce(f32[34,34]{1,0:T(8,128)S(1)} %fusion.30), channel_id=1, replica_groups=mesh['pairs'=2,'src'=8,'tgt'=2] {'src','tgt'}, use_global_device_ids=true, to_apply=%region_15.16 | all-reduce | flops 1156 | bytes 9248 | tf_op jit(solution)/shard_map/psum | solution.py:81
  (35 shorter events, 7.0 us)
Async XLA Ops:
  0.6 20.9 %copy-start = (f32[34,34]{1,0:T(8,128)S(1)}, f32[34,34]{1,0:T(8,128)}, u32[]{:S(2)}) copy-start(f32[34,34]{1,0:T(8,128)} %param.7) | copy-start | bytes 13876
  0.6 9.2 %collective-permute-start = (f32[8192,4]{0,1:T(4,128)}, f32[8192,4]{0,1:T(4,128)S(1)}, u32[]{:S(2)}, u32[]{:S(2)}) collective-permute-start(f32[8192,4]{0,1:T(4,128)} %param.5), channel_id=1, source_target_pairs={{0,14},{2,0},{4,2},{6,4},{8,6},{10,8},{12,10},{14,12},{1,15},{3,1}... | collective-permute-start | bytes 393224 | tf_op jit(solution)/shard_map/ppermute | solution.py:16
  10.8 7.2 %collective-permute-start.1 = (f32[8192,8]{0,1:T(8,128)S(1)}, f32[8192,8]{0,1:T(8,128)S(1)}, u32[]{:S(2)}, u32[]{:S(2)}) collective-permute-start(f32[8192,8]{0,1:T(8,128)S(1)} %pad_maximum_fusion.7), channel_id=1, source_target_pairs={{0,12},{2,14},{4,0},{6,2},{8,4},{10,6},{12,8},{14,10},{1,13},{3,15... | collective-permute-start | bytes 786440 | tf_op jit(solution)/shard_map/ppermute | solution.py:16
  19.0 24.2 %collective-permute-start.2 = (f32[8192,16]{0,1:T(8,128)S(1)}, f32[8192,16]{0,1:T(8,128)S(1)}, u32[]{:S(2)}, u32[]{:S(2)}) collective-permute-start(f32[8192,16]{0,1:T(8,128)S(1)} %pad_maximum_fusion.6), channel_id=1, source_target_pairs={{0,8},{2,10},{4,12},{6,14},{8,0},{10,2},{12,4},{14,6},{1,9},{3,11}... | collective-permute-start | bytes 1572872 | tf_op jit(solution)/shard_map/ppermute | solution.py:16
  21.8 24.9 %copy-start.4 = (f32[8192]{0:T(1024)S(1)}, f32[8192]{0:T(1024)}, u32[]{:S(2)}) copy-start(f32[8192]{0:T(1024)} %param.6) | copy-start | bytes 98308
  50.5 5.8 %copy-start.2 = (f32[128,8192]{1,0:T(8,128)}, f32[128,8192]{1,0:T(8,128)S(1)}, u32[]{:S(2)}) copy-start(f32[128,8192]{1,0:T(8,128)S(1)} %get-tuple-element.38) | copy-start | bytes 12582916
  55.2 54.8 %copy-start.3 = (f32[8192,32]{0,1:T(8,128)S(1)}, f32[8192,32]{0,1:T(8,128)}, u32[]{:S(2)}) copy-start(f32[8192,32]{0,1:T(8,128)} %get-tuple-element.27) | copy-start | bytes 3145732
  56.3 13.0 %all-to-all-start = ((f32[1,8,1024]{2,0,1:T(1,128)}), f32[1,8,1024]{2,0,1:T(1,128)S(1)}, u32[]{:S(2)}, u32[]{:S(2)}) async-start(f32[1,8,1024]{2,0,1:T(1,128)} %bitcast.8), calls=%async_computation | async-start | bytes 65536 | tf_op jit(solution)/shard_map/all_to_all | solution.py:71
  69.4 10.0 %all-to-all-start.1 = ((f32[1,8,1024]{2,0,1:T(1,128)}), f32[1,8,1024]{2,0,1:T(1,128)S(1)}, u32[]{:S(2)}, u32[]{:S(2)}) async-start(f32[1,8,1024]{2,0,1:T(1,128)} %bitcast.9), calls=%async_computation.1 | async-start | bytes 65536 | tf_op jit(solution)/shard_map/all_to_all | solution.py:72
  178.3 5.8 %copy-start.1 = (f32[128,8192]{1,0:T(8,128)}, f32[128,8192]{1,0:T(8,128)S(1)}, u32[]{:S(2)}) copy-start(f32[128,8192]{1,0:T(8,128)S(1)} %get-tuple-element.40) | copy-start | bytes 12582916
  182.9 51.8 %copy-start.5 = (f32[128]{0:T(128)}, f32[128]{0:T(128)S(1)}, u32[]{:S(2)}) copy-start(f32[128]{0:T(128)S(1)} %multiply_subtract_fusion.2) | copy-start | bytes 1540
  184.1 10.0 %all-to-all-start.2 = ((f32[1,8,1024]{2,0,1:T(1,128)}), f32[1,8,1024]{2,0,1:T(1,128)S(1)}, u32[]{:S(2)}, u32[]{:S(2)}) async-start(f32[1,8,1024]{2,0,1:T(1,128)} %bitcast.16), calls=%async_computation.2 | async-start | bytes 65536 | tf_op jit(solution)/shard_map/all_to_all | solution.py:71
  194.1 10.0 %all-to-all-start.3 = ((f32[1,8,1024]{2,0,1:T(1,128)}), f32[1,8,1024]{2,0,1:T(1,128)S(1)}, u32[]{:S(2)}, u32[]{:S(2)}) async-start(f32[1,8,1024]{2,0,1:T(1,128)} %bitcast.17), calls=%async_computation.3 | async-start | bytes 65536 | tf_op jit(solution)/shard_map/all_to_all | solution.py:72
